TPU v7x, 32 devices: a whole 2x2x4 slice. The times are simulated.
32 devices in a mesh: rows: 8 (over z, y), cols: 4 (over x, core).
Axes of the slice: x: 2, y: 2, z: 4, core: 2. Of those that a mesh axis runs over, the one named last changes fastest.
Arguments:
- coefficients: float32 [4, 1024, 4, 256], P(None, 'rows'), may hold values from -0.03 to 0.09
- support: int32 [4, 1024, 4], P(None, 'rows'), may hold values from 0 to 11, all different within a row
- primal: float32 [12, 256, 256], P('cols'), may hold values from -0.5 to 9, as said below
- dual_inverse: float32 [12, 256, 256], P('cols'), may hold values from -0.5 to 9, as said below
- block_sizes: int32 [12], P('cols'), may hold values from 64 to 256, as said below
- damping: float32 [4, 1024], P(None, 'rows'), may hold values from 0.5 to 2
- right_sides: float32 [4, 32, 1024], P(None, 'cols', 'rows'), may hold values from -6 to 6
Outputs:
- updated: float32 [4, 1024, 4096], P(None, 'rows', 'cols')
- panel_factor: float32 [4, 1024, 128], P(None, 'rows')
- solved: float32 [4, 32, 1024], P(None, 'cols', 'rows')
Inputs may be any that keep to these rules, and one draw needn't show every extreme that they name: `primal`: each block is symmetric positive definite. `dual_inverse`: each block is symmetric positive definite. `block_sizes`: some block has order 256.
All inputs are finite; a program needn't handle non-finite values.
Results may differ from a plain program's by a relative error of at most 0.00015.
Values sent between devices are 32-bit elements; how exact they have to be, the bound alone decides.
A program may use at most 192 MiB of HBM per device.

v0:
```python
import functools

import jax
import jax.numpy as jnp
from jax import lax
from jax.experimental import pallas as pl
from jax.experimental.pallas import tpu as pltpu
from jax.sharding import PartitionSpec as P

TILE = 128

MESH = pl.DeviceIdType.MESH
highest = lax.Precision.HIGHEST


def split(x):
    top = x.astype(jnp.bfloat16)
    return top, (x - top.astype(jnp.float32)).astype(jnp.bfloat16)


def product(a, b, dims):
    return lax.dot_general(a, b, (dims, ((), ())), preferred_element_type=jnp.float32)


def three(a_top, a_low, b_top, b_low, dims):
    return product(a_top, b_top, dims) + (product(a_top, b_low, dims) + product(a_low, b_top, dims))


def select_block(coef, label, b):
    pieces = []
    for h in range(0, 2):
        acc = None
        for k in range(coef.slots):
            hit = label(k) == b
            value = coef(k, h)
            acc = jnp.where(hit, value, jnp.zeros_like(value) if acc is None else acc)
        pieces.append(acc)
    return jnp.concatenate(pieces, axis=1)


class Rows:
    def __init__(self, read, slots):
        self.read, self.slots = read, slots

    def __call__(self, k, h):
        return self.read(k, pl.ds(h * TILE, TILE))


def exchange(rows, cols, tile_ref, names_ref, lead_ref, small_ref, w_ref, own_ref, own_names_ref,
             schur_out, lead_schur_out, inverse_out, small_out,
             tiles_out, names_out, leads_out, w_out, label_own, label_col, lead_sc, d_top, d_low, c_top, c_low,
             g_top, g_low, acc, work,
             local_sem, fwd_s, fwd_r, bwd_s, bwd_r, name_s, name_r, lead_s, lead_r, share_s, share_r, small_s, small_r,
             wx_s, wx_r, wp_s, wp_r):
    r = lax.axis_index("rows")
    c = lax.axis_index("cols")
    half = rows // 2
    odd = r % 2
    pos = (1 - odd) * (r // 2) + odd * (rows - 1 - r // 2)

    def row_at(p):
        p = (p + rows) % rows
        upper = p // half
        return (1 - upper) * (2 * p) + upper * (2 * (rows - 1 - p) + 1)

    right = row_at(pos + 1)
    left = row_at(pos - 1)
    partner = c + 1 - 2 * (c % 2)

    def send(src, dst, s, v, row=None, col=None):
        return pltpu.make_async_remote_copy(
            src_ref=src, dst_ref=dst, send_sem=s, recv_sem=v,
            device_id=(r if row is None else row, c if col is None else col), device_id_type=MESH)

    barrier = pltpu.get_barrier_semaphore()
    for d in range(1, rows):
        pl.semaphore_signal(barrier, inc=1, device_id=((r + d) % rows, c), device_id_type=MESH)
    for d in range(1, cols):
        pl.semaphore_signal(barrier, inc=1, device_id=(r, (c + d) % cols), device_id_type=MESH)
    pl.semaphore_wait(barrier, rows + cols - 2)

    own_blocks = w_ref.shape[0]
    blocks = w_out.shape[0]
    height = own_ref.shape[1]
    slots = tile_ref.shape[0]
    cut = slots // 2
    part = (pl.ds(0, cut), pl.ds(cut, slots - cut))

    own = [pltpu.make_async_copy(tile_ref, tiles_out.at[r], local_sem.at[0]),
           pltpu.make_async_copy(names_ref, names_out.at[r], local_sem.at[1]),
           pltpu.make_async_copy(w_ref, w_out.at[pl.ds(c * own_blocks, own_blocks)], local_sem.at[2])]
    for copy in own:
        copy.start()

    waits = []
    for k in range(1, cols // 2):
        copy = send(w_ref, w_out.at[pl.ds(c * own_blocks, own_blocks)], wx_s.at[k], wx_r.at[k], col=(c + 2 * k) % cols)
        copy.start()
        waits.append(copy)
    copy = send(w_ref, w_out.at[pl.ds(c * own_blocks, own_blocks)], wp_s.at[0], wp_r.at[0], col=partner)
    copy.start()
    waits.append(copy)

    for d in range(1, rows):
        copy = send(names_ref, names_out.at[r], name_s.at[d], name_r.at[d], row=(r + d) % rows)
        copy.start()
        waits.append(copy)

    lead_row = [send(lead_ref, leads_out.at[c], lead_s.at[0], lead_r.at[0], row=right),
                send(lead_ref, leads_out.at[c], lead_s.at[1], lead_r.at[0], row=left)]

    @pl.when(r == 0)
    def _():
        for copy in lead_row:
            copy.start()
        for d in range(1, rows):
            send(small_ref, small_out, small_s.at[d], small_r.at[0], row=d).start()
        pltpu.make_async_copy(lead_ref, leads_out.at[c], local_sem.at[3]).start()
        pltpu.make_async_copy(small_ref, small_out, local_sem.at[4]).start()

    def first(h):
        send(tile_ref.at[part[h]], tiles_out.at[r, part[h]], fwd_s.at[0, h], fwd_r.at[0, h], row=right).start()
        send(tile_ref.at[part[h]], tiles_out.at[r, part[h]], bwd_s.at[0, h], bwd_r.at[0, h], row=left).start()

    first(0)
    near = jnp.minimum(pos, rows - pos)

    @pl.when(near >= 2)
    def _():
        first(1)

    def put_labels(dst, at, names):
        turned = jnp.transpose(names)
        for k in range(slots):
            dst[k, pl.ds(at, TILE), :] = jnp.broadcast_to(turned[:, k:k + 1], (TILE, TILE))

    for t in range(height // TILE):
        put_labels(label_own, t * TILE, own_names_ref[t])

    relay_right = send(leads_out.at[c], leads_out.at[c], lead_s.at[0], lead_r.at[0], row=right)
    relay_left = send(leads_out.at[c], leads_out.at[c], lead_s.at[1], lead_r.at[0], row=left)

    @pl.when(r != 0)
    def _():
        relay_right.wait_recv()

    @pl.when((pos >= 1) & (pos < half))
    def _():
        relay_right.start()

    @pl.when(pos >= half + 2)
    def _():
        relay_left.start()

    @pl.when(r == 0)
    def _():
        pltpu.make_async_copy(lead_ref, leads_out.at[c], local_sem.at[3]).wait()
        pltpu.make_async_copy(small_ref, small_out, local_sem.at[4]).wait()

    for d in range(1, cols):
        copy = send(leads_out.at[c], leads_out.at[c], share_s.at[d], share_r.at[d], col=(c + d) % cols)
        copy.start()
        waits.append(copy)

    @pl.when(near < 2)
    def _():
        first(1)

    last = half - 1

    def ring(s, h):
        ahead = row_at(pos - s)
        behind = row_at(pos + s)
        send(tile_ref.at[part[h]], tiles_out.at[r, part[h]], fwd_s.at[s - 1, h], fwd_r.at[s - 1, h], row=right).wait_recv()
        if s < last or h == 0:
            send(tiles_out.at[ahead, part[h]], tiles_out.at[ahead, part[h]], fwd_s.at[s, h], fwd_r.at[s, h], row=right).start()
        send(tile_ref.at[part[h]], tiles_out.at[r, part[h]], bwd_s.at[s - 1, h], bwd_r.at[s - 1, h], row=left).wait_recv()
        if s < last or h == 1:
            send(tiles_out.at[behind, part[h]], tiles_out.at[behind, part[h]], bwd_s.at[s, h], bwd_r.at[s, h], row=left).start()

    pending = [(s, h) for s in range(1, half) for h in range(2)]

    def serve(count):
        for _ in range(count):
            if pending:
                ring(*pending.pop(0))

    serve(2)
    for k in range(1, cols // 2):
        send(w_ref, w_out.at[pl.ds(c * own_blocks, own_blocks)], wx_s.at[k], wx_r.at[k], col=(c + 2 * k) % cols).wait_recv()
        source = (c + cols - 2 * k) % cols
        span = pl.ds(source * own_blocks, own_blocks)
        copy = send(w_out.at[span], w_out.at[span], wp_s.at[k], wp_r.at[k], col=partner)
        copy.start()
        waits.append(copy)
    for d in range(1, cols):
        send(leads_out.at[c], leads_out.at[c], share_s.at[d], share_r.at[d], col=(c + d) % cols).wait_recv()

    @pl.when(r != 0)
    def _():
        send(small_ref, small_out, small_s.at[0], small_r.at[0], row=0).wait_recv()

    for d in range(1, rows):
        send(names_ref, names_out.at[r], name_s.at[d], name_r.at[d], row=(r + d) % rows).wait_recv()
    for copy in own:
        copy.wait()
    chunk = TILE // cols
    for q in range(cols):
        lead_sc[:, q * chunk:(q + 1) * chunk, :] = leads_out[q]
    put_labels(label_own, height, small_out[0:8, :])
    for k in range(cols // 2):
        send(w_ref, w_out.at[pl.ds(c * own_blocks, own_blocks)], wp_s.at[k], wp_r.at[k], col=partner).wait_recv()
    serve(1)

    def weigh(b, carry):
        name = b.astype(jnp.float32)
        for t in range(height // TILE + 1):
            at = pl.ds(t * TILE, TILE)
            if t < height // TILE:
                coef = Rows(lambda k, lanes: own_ref[k, at, lanes], slots)
            else:
                coef = Rows(lambda k, lanes: lead_sc[k, :, lanes], slots)
            top, low = split(select_block(coef, lambda k: label_own[k, at, :], name))
            d_top[at, :] = top
            d_low[at, :] = low
        w_top, w_low = split(w_out[b])
        top, low = split(three(d_top[...], d_low[...], w_top, w_low, ((1,), (0,))))
        g_top[b] = top
        g_low[b] = low
        return carry

    middle = blocks // 2
    lax.fori_loop(0, middle, weigh, 0)
    serve(1)
    lax.fori_loop(middle, blocks, weigh, 0)
    serve(1)

    def group(tiles):
        width = len(tiles) * TILE
        for i, row in enumerate(tiles):
            put_labels(label_col, i * TILE, small_out[0:8, :] if row is None else names_out[row])
        acc[:, :width] = jnp.zeros((acc.shape[0], width), jnp.float32)

        def body(b, carry):
            name = b.astype(jnp.float32)
            for i, row in enumerate(tiles):
                at = pl.ds(i * TILE, TILE)
                if row is None:
                    coef = Rows(lambda k, lanes: lead_sc[k, :, lanes], slots)
                else:
                    coef = Rows(lambda k, lanes: tiles_out[row, k, :, lanes], slots)
                top, low = split(select_block(coef, lambda k: label_col[k, at, :], name))
                c_top[at, :] = top
                c_low[at, :] = low
            acc[:, :width] += three(g_top[b], g_low[b], c_top[:width, :], c_low[:width, :], ((1,), (1,)))
            return carry

        lax.fori_loop(0, blocks, body, 0)
        for i, row in enumerate(tiles):
            value = acc[:, i * TILE:(i + 1) * TILE]
            if row is None:
                lead_schur_out[...] = value
            else:
                schur_out[:, pl.ds(pl.multiple_of(row * TILE, TILE), TILE)] = value

    group([None, r])
    serve(1)

    lane = lax.broadcasted_iota(jnp.int32, (TILE, TILE), 1)
    line = lax.broadcasted_iota(jnp.int32, (TILE, TILE), 0)
    work[:, :TILE] = lead_schur_out[height:, :] + jnp.where(lane == line, jnp.broadcast_to(small_out[7:8, :], (TILE, TILE)), 0.0)
    work[:, TILE:] = jnp.where(lane == line, 1.0, 0.0)

    def eliminate(j, carry):
        pivot = work[pl.ds(j, 1), :]
        column = jnp.sum(jnp.where(lane == j, work[:, :TILE], 0.0), axis=1, keepdims=True)
        scale = jnp.sum(jnp.where(lane[0:1] == j, pivot[:, :TILE], 0.0), axis=1, keepdims=True)
        factor = jnp.where(line[:, 0:1] > j, column, 0.0) / scale
        work[...] = work[...] - factor * pivot
        return carry

    lax.fori_loop(0, TILE // 2, eliminate, 0)
    serve(1)
    lax.fori_loop(TILE // 2, TILE, eliminate, 0)
    diagonal = jnp.sum(jnp.where(lane == line, work[:, :TILE], 0.0), axis=1, keepdims=True)
    inverse_out[...] = work[:, TILE:] / jnp.sqrt(diagonal)

    for g in range(1, half):
        while pending and pending[0][0] <= g:
            serve(1)
        group([row_at(pos - g), row_at(pos + g)])
        serve(2)
    send(tile_ref.at[part[0]], tiles_out.at[r, part[0]], fwd_s.at[last, 0], fwd_r.at[last, 0], row=right).wait_recv()
    send(tile_ref.at[part[1]], tiles_out.at[r, part[1]], bwd_s.at[last, 1], bwd_r.at[last, 1], row=left).wait_recv()
    group([row_at(pos + half)])

    for s in range(half):
        for h in range(2):
            if s < last or h == 0:
                send(tile_ref.at[part[h]], tiles_out.at[r, part[h]], fwd_s.at[s, h], fwd_r.at[s, h], row=right).wait_send()
            if s < last or h == 1:
                send(tile_ref.at[part[h]], tiles_out.at[r, part[h]], bwd_s.at[s, h], bwd_r.at[s, h], row=left).wait_send()

    for copy in waits:
        copy.wait_send()
    @pl.when(r == 0)
    def _():
        for copy in lead_row:
            copy.wait_send()
        for d in range(1, rows):
            send(small_ref, small_out, small_s.at[d], small_r.at[0], row=d).wait_send()

    @pl.when((pos >= 1) & (pos < half))
    def _():
        relay_right.wait_send()

    @pl.when(pos >= half + 2)
    def _():
        relay_left.wait_send()


def assemble(rows, cols, tile, names, lead, small, weights, own, own_names):
    half = rows // 2
    dma = pltpu.SemaphoreType.DMA
    vmem = pl.BlockSpec(memory_space=pltpu.VMEM)
    slots, height, order = own.shape
    blocks = cols * weights.shape[0]
    tall = height + TILE
    f32, bf16 = jnp.float32, jnp.bfloat16
    return pl.pallas_call(
        functools.partial(exchange, rows, cols),
        out_shape=[
            jax.ShapeDtypeStruct((tall, rows * TILE), f32),
            jax.ShapeDtypeStruct((tall, TILE), f32),
            jax.ShapeDtypeStruct((TILE, TILE), f32),
            jax.ShapeDtypeStruct(small.shape, f32),
        ],
        in_specs=[vmem] * 7,
        out_specs=[vmem] * 4,
        scratch_shapes=[
            pltpu.VMEM((rows,) + tile.shape, f32),
            pltpu.VMEM((rows,) + names.shape, f32),
            pltpu.VMEM((cols,) + lead.shape, f32),
            pltpu.VMEM((blocks, order, order), f32),
            pltpu.VMEM((slots, tall, TILE), f32),
            pltpu.VMEM((slots, 2 * TILE, TILE), f32),
            pltpu.VMEM((slots, TILE, order), f32),
            pltpu.VMEM((tall, order), bf16),
            pltpu.VMEM((tall, order), bf16),
            pltpu.VMEM((2 * TILE, order), bf16),
            pltpu.VMEM((2 * TILE, order), bf16),
            pltpu.VMEM((blocks, tall, order), bf16),
            pltpu.VMEM((blocks, tall, order), bf16),
            pltpu.VMEM((tall, 2 * TILE), f32),
            pltpu.VMEM((TILE, 2 * TILE), f32),
        ]
        + [dma((5,))] + [dma((half, 2))] * 4 + [dma((rows,))] * 2 + [dma((2,)), dma((1,))]
        + [dma((cols,))] * 2 + [dma((rows,)), dma((1,))] + [dma((cols,))] * 4,
        compiler_params=pltpu.CompilerParams(collective_id=0, has_side_effects=True),
    )(tile, names, lead, small, weights, own, own_names)


def local(coefficients, support, primal, dual_inverse, block_sizes, damping, right_sides):
    col_index = lax.axis_index("cols")
    row_index = lax.axis_index("rows")
    rows = lax.axis_size("rows")
    cols = lax.axis_size("cols")
    layers, _, slots, order = coefficients.shape
    span = TILE * rows
    count_all = layers * span
    col_width = count_all // cols
    sides = right_sides.shape[1]
    positions = jnp.arange(order, dtype=jnp.int32)
    active = (positions[None, :] < block_sizes[:, None]).astype(jnp.float32)
    weights = primal * dual_inverse * active[:, :, None] * active[:, None, :]

    layer = (col_index * col_width) // span
    tile = jnp.transpose(lax.dynamic_index_in_dim(coefficients, layer, 0, keepdims=False), (1, 0, 2))
    own_names = jnp.pad(jnp.transpose(support, (0, 2, 1)).astype(jnp.float32), ((0, 0), (0, 8 - slots), (0, 0)))
    names = lax.dynamic_index_in_dim(own_names, layer, 0, keepdims=False)
    chunk = TILE // cols
    lead = jnp.transpose(lax.dynamic_slice_in_dim(coefficients[0], col_index * chunk, chunk, 0), (1, 0, 2))
    small = jnp.concatenate([
        own_names[0][:7],
        damping[0][None, :],
        jnp.pad(right_sides[0], ((0, -sides % 8), (0, 0)))], axis=0)
    own = jnp.transpose(coefficients, (2, 0, 1, 3)).reshape(slots, layers * TILE, order)
    schur_rows, own_lead, inverse, small = assemble(rows, cols, tile, names, lead, small, weights, own, own_names)
    if span != col_width:
        schur_rows = lax.dynamic_slice_in_dim(schur_rows, (col_index * col_width) % span, col_width, 1)
    lead_damping = small[7]
    top_sides = small[8:8 + sides]

    row_global = ((jnp.arange(layers)[:, None] * rows + row_index) * TILE + jnp.arange(TILE)[None, :]).reshape(-1)
    col_global = col_index * col_width + jnp.arange(col_width)
    flat_damping = damping.reshape(-1)
    schur = schur_rows[:layers * TILE] + jnp.where(row_global[:, None] == col_global[None, :], flat_damping[:, None], 0.0)
    lead_ids = jnp.arange(TILE)
    panel_raw = own_lead[:layers * TILE] + jnp.where(row_global[:, None] == lead_ids[None, :], flat_damping[:, None], 0.0)
    column_raw = schur_rows[layers * TILE:] + jnp.where(lead_ids[:, None] == col_global[None, :], lead_damping[:, None], 0.0)
    panel_factor = jnp.einsum("ak,jk->aj", panel_raw, inverse, precision=highest)
    column_panel = jnp.einsum("jk,kn->jn", inverse, column_raw, precision=highest)
    outer_term = jnp.dot(panel_factor, column_panel, precision=highest)
    row_later = row_global >= TILE
    col_later = col_global >= TILE
    updated = schur - jnp.where(row_later[:, None] & col_later[None, :], outer_term, 0.0)
    leading = jnp.einsum("sk,jk->sj", top_sides, inverse, precision=highest)
    panel_factor = panel_factor.reshape(layers, TILE, TILE)
    remainder = right_sides - jnp.einsum("sk,tak->tsa", leading, panel_factor, precision=highest)
    solved = jnp.where(row_later.reshape(layers, TILE)[:, None, :], remainder, leading[None, :, :])
    return (updated.reshape(layers, TILE, col_width), panel_factor, solved)


def solution(mesh):
    in_specs = (
        P(None, "rows", None, None),
        P(None, "rows", None),
        P("cols", None, None),
        P("cols", None, None),
        P("cols"),
        P(None, "rows"),
        P(None, "cols", "rows"),
    )
    out_specs = (P(None, "rows", "cols"), P(None, "rows", None), P(None, "cols", "rows"))
    return jax.shard_map(local, mesh=mesh, in_specs=in_specs, out_specs=out_specs, check_vma=False)
```

profile of v0, /device:TPU:22, one launch (start us, length us, event | category | flops | bytes accessed | tf_op | source)
XLA Modules:
  0.0 107.1 jit_solution(7462290470273510028)
XLA Ops:
  0.6 0.0 copy-start
  0.6 0.0 copy-start.6
  0.7 0.0 copy-start.4
  0.7 0.0 slice-start
  0.7 1.5 %fusion.26 = (f32[1,128,4,256]{3,2,1,0:T(4,128)S(1)}, f32[1,128,4,256]{3,2,1,0:T(4,128)S(1)}) fusion(f32[4,128,4,256]{3,2,1,0:T(4,128)} %param.7, s32[]{:T(128)S(6)} %select_n.35), kind=kLoop, calls=%fused_computation.47 | loop fusion | bytes 2097156 | tf_op jit(solution)/shard_map/slice | solution.py:382
  2.2 0.9 copy.15
  3.1 0.7 copy.16
  3.8 0.0 copy-done.6
  3.8 0.6 fusion.16.names_ref
  4.4 0.0 copy-done.4
  4.4 0.0 slice-done
  4.4 0.6 pad_maximum_fusion.small_ref
  5.0 0.6 pad.4.own_names_ref
  5.6 0.0 copy-done
  5.6 0.0 copy-start.7
  5.6 0.0 copy-start.2
  5.6 0.0 copy-start.3
  5.6 1.7 %copy.12 = f32[4,4,128,256]{3,2,1,0:T(8,128)} copy(f32[4,4,128,256]{3,0,2,1:T(4,128)S(1)} %bitcast.45) | data formatting | bytes 4194304 | tf_op jit(solution)/shard_map/transpose | solution.py:387
  7.3 0.0 copy-done.7
  7.3 0.1 fusion.21
  7.4 0.0 copy-done.2
  7.4 0.0 copy-done.3
  7.4 1.1 %multiply_multiply_fusion.w_ref = f32[3,256,256]{2,1,0:T(8,128)} fusion(f32[3,256,256]{2,1,0:T(8,128)S(1)} %copy-done.2, f32[3,256,256]{2,1,0:T(8,128)S(1)} %copy-done.3, f32[3,256]{1,0:T(4,128)S(1)} %fusion.21), kind=kLoop, calls=%fused_computation.4 | loop fusion | flops 589824 | bytes 2362368 | tf_op jit(solution)/shard_map/mul | solution.py:375
  8.5 0.0 copy-start.5
  8.5 87.4 %shard_map.94 = (f32[640,1024]{1,0:T(8,128)}, f32[640,128]{1,0:T(8,128)}, f32[128,128]{1,0:T(8,128)}, f32[16,128]{1,0:T(8,128)}) custom-call(f32[4,128,256]{2,1,0:T(8,128)} %bitcast.49, f32[8,128]{1,0:T(8,128)} %fusion.16.names_ref, f32[4,32,256]{2,1,0:T(8,128)} %bitcast.50, f32[16,128]{1,0:T(8,128)} %pad_maximum_fusion.small_ref, ...), custom_call_target="tpu_custom_call" | custom-call | tf_op jit(solution)/shard_map/pallas_call | solution.py:330
  95.9 1.0 fusion.19
  96.9 0.1 fusion.23
  97.0 0.0 copy-done.5
  97.0 1.4 %fusion.9 = f32[512,128]{1,0:T(8,128)S(1)} fusion(f32[128,128]{1,0:T(8,128)} %get-tuple-element.9, f32[640,128]{1,0:T(8,128)} %get-tuple-element.8, f32[512]{0:T(512)S(1)} %bitcast.51, s32[512]{0:T(512)S(1)} %fusion.23), kind=kOutput, calls=%fused_computation.14 | convolution fusion | flops 100859904 | bytes 593920 | tf_op jit(solution)/shard_map/ak,jk->aj/dot_general | solution.py:401
  98.4 0.0 copy-start.1
  98.4 0.1 fusion.22
  98.5 0.9 fusion.1
  99.5 0.7 slice_bitcast_fusion.1
  100.1 1.8 %fusion.2 = f32[128,1024]{1,0:T(8,128)S(1)} fusion(f32[128,128]{1,0:T(8,128)} %get-tuple-element.9, f32[640,1024]{1,0:T(8,128)} %get-tuple-element.7, f32[128]{0:T(128)S(1)} %slice_bitcast_fusion.1, s32[1024]{0:T(1024)S(1)} %iota_add_fusion), kind=kOutput, calls=%fused_computation.6 | convolution fusion | flops 201719808 | bytes 1118720 | tf_op jit(solution)/shard_map/jk,kn->jn/dot_general | solution.py:402
  102.0 0.1 broadcast_compare_fusion.1
  102.0 5.1 %select_subtract_fusion = f32[512,1024]{1,0:T(8,128)} fusion(f32[640,1024]{1,0:T(8,128)} %get-tuple-element.7, f32[512,128]{1,0:T(8,128)S(1)} %fusion.9, f32[128,1024]{1,0:T(8,128)S(1)} %fusion.2, f32[512]{0:T(512)S(1)} %bitcast.52, s32[1024]{0:T(1024)S(1)} %iota_add_fusion, s32[512]{0:T(512)S(1)} %fusion.23, pred[1024]{0:T(1024)(128)(4,1)S(1)} %broadcast_compare_fusion, ...), kind=kOutput, calls=%fused_computation | convolution fusion | flops 808452096 | bytes 4990464 | tf_op jit(solution)/shard_map/dot_general | solution.py:403
  107.1 0.0 copy-done.1
  (7 shorter events, 0.0 us)
Async XLA Ops:
  0.6 5.0 %copy-start = (f32[4,128,4,256]{3,2,1,0:T(4,128)S(1)}, f32[4,128,4,256]{3,2,1,0:T(4,128)}, u32[]{:S(2)}) copy-start(f32[4,128,4,256]{3,2,1,0:T(4,128)} %param.7) | copy-start | bytes 6291460
  0.6 3.2 %copy-start.6 = (s32[4,128,4]{1,2,0:T(4,128)S(1)}, s32[4,128,4]{1,2,0:T(4,128)}, u32[]{:S(2)}) copy-start(s32[4,128,4]{1,2,0:T(4,128)} %param.8) | copy-start | bytes 24580
  0.7 3.8 %copy-start.4 = (f32[4,8,128]{2,1,0:T(8,128)S(1)}, f32[4,8,128]{2,1,0:T(8,128)}, u32[]{:S(2)}) copy-start(f32[4,8,128]{2,1,0:T(8,128)} %param.13) | copy-start | bytes 49156
  0.7 3.8 %slice-start = ((f32[4,128]{1,0:T(4,128)}), f32[1,128]{1,0:T(1,128)S(1)}, s32[]{:S(2)}) async-start(f32[4,128]{1,0:T(4,128)} %param.12), calls=%async_computation | async-start | bytes 1024 | tf_op jit(solution)/shard_map/slice | solution.py:385
  5.6 1.7 %copy-start.7 = (s32[3]{0:T(128)S(1)}, s32[3]{0:T(128)}, u32[]{:S(2)}) copy-start(s32[3]{0:T(128)} %param.11) | copy-start | bytes 40
  5.6 1.8 %copy-start.2 = (f32[3,256,256]{2,1,0:T(8,128)S(1)}, f32[3,256,256]{2,1,0:T(8,128)}, u32[]{:S(2)}) copy-start(f32[3,256,256]{2,1,0:T(8,128)} %param.9) | copy-start | bytes 2359300
  5.6 1.8 %copy-start.3 = (f32[3,256,256]{2,1,0:T(8,128)S(1)}, f32[3,256,256]{2,1,0:T(8,128)}, u32[]{:S(2)}) copy-start(f32[3,256,256]{2,1,0:T(8,128)} %param.10) | copy-start | bytes 2359300
  8.5 88.5 %copy-start.5 = (f32[4,128]{1,0:T(4,128)S(1)}, f32[4,128]{1,0:T(4,128)}, u32[]{:S(2)}) copy-start(f32[4,128]{1,0:T(4,128)} %param.12) | copy-start | bytes 6148
  98.4 8.7 %copy-start.1 = (f32[512,128]{1,0:T(8,128)}, f32[512,128]{1,0:T(8,128)S(1)}, u32[]{:S(2)}) copy-start(f32[512,128]{1,0:T(8,128)S(1)} %fusion.9) | copy-start | bytes 786436
where the time goes:
time: 109 us; the launch traced here: 107 us
  Pallas kernels  87.4 us (80%)
  matrix products  10.2 us (9%)
  local copies, waits for them, and re-layouts  6.73 us (6%)
  other arithmetic  2 us (2%)
    pallas_call x1, Pallas kernels, assemble(): pl.pallas_call(functools.partial(exchange, rows, cols), out_shape=[jax.Sh...  87.4 us
    dot_general x1, matrix products, local(): outer_term = jnp.dot(panel_factor, column_panel, precision=highest)  5.08 us

commit v1 on v0

--- a/solution.py
+++ b/solution.py
@@ -46,7 +46,7 @@
         return self.read(k, pl.ds(h * TILE, TILE))
 
 
-def exchange(rows, cols, tile_ref, names_ref, lead_ref, small_ref, w_ref, own_ref, own_names_ref,
+def exchange(rows, cols, small_ref, w_ref, own_ref, own_names_ref,
              schur_out, lead_schur_out, inverse_out, small_out,
              tiles_out, names_out, leads_out, w_out, label_own, label_col, lead_sc, d_top, d_low, c_top, c_low,
              g_top, g_low, acc, work,
@@ -82,24 +82,32 @@
     own_blocks = w_ref.shape[0]
     blocks = w_out.shape[0]
     height = own_ref.shape[1]
-    slots = tile_ref.shape[0]
+    slots = own_ref.shape[0]
+    layer = (c * (height * rows // cols)) // (rows * TILE)
+    tile_ref = own_ref.at[:, pl.ds(pl.multiple_of(layer * TILE, TILE), TILE)]
+    names_ref = own_names_ref.at[layer]
+    chunk = TILE // cols
+    lead_ref = own_ref.at[:, pl.ds(pl.multiple_of(c * chunk, chunk), chunk)]
     cut = slots // 2
     part = (pl.ds(0, cut), pl.ds(cut, slots - cut))
 
     own = [pltpu.make_async_copy(tile_ref, tiles_out.at[r], local_sem.at[0]),
-           pltpu.make_async_copy(names_ref, names_out.at[r], local_sem.at[1]),
-           pltpu.make_async_copy(w_ref, w_out.at[pl.ds(c * own_blocks, own_blocks)], local_sem.at[2])]
+           pltpu.make_async_copy(names_ref, names_out.at[r], local_sem.at[1])]
     for copy in own:
         copy.start()
 
     waits = []
-    for k in range(1, cols // 2):
-        copy = send(w_ref, w_out.at[pl.ds(c * own_blocks, own_blocks)], wx_s.at[k], wx_r.at[k], col=(c + 2 * k) % cols)
+    def weight(source, i):
+        return w_out.at[source * own_blocks + i]
+
+    for i in range(own_blocks):
+        copy = send(w_ref.at[i], weight(c, i), wp_s.at[0, i], wp_r.at[0, i], col=partner)
         copy.start()
         waits.append(copy)
-    copy = send(w_ref, w_out.at[pl.ds(c * own_blocks, own_blocks)], wp_s.at[0], wp_r.at[0], col=partner)
-    copy.start()
-    waits.append(copy)
+        for k in range(1, cols // 2):
+            copy = send(w_ref.at[i], weight(c, i), wx_s.at[k, i], wx_r.at[k, i], col=(c + 2 * k) % cols)
+            copy.start()
+            waits.append(copy)
 
     for d in range(1, rows):
         copy = send(names_ref, names_out.at[r], name_s.at[d], name_r.at[d], row=(r + d) % rows)
@@ -136,6 +144,42 @@
 
     for t in range(height // TILE):
         put_labels(label_own, t * TILE, own_names_ref[t])
+    full = height // TILE
+
+    def arrived(k, i):
+        send(w_ref.at[i], weight(c, i), wp_s.at[k, i], wp_r.at[k, i], col=partner).wait_recv()
+
+    def forward(i):
+        if i < own_blocks:
+            for k in range(1, cols // 2):
+                send(w_ref.at[i], weight(c, i), wx_s.at[k, i], wx_r.at[k, i], col=(c + 2 * k) % cols).wait_recv()
+                source = (c + cols - 2 * k) % cols
+                copy = send(weight(source, i), weight(source, i), wp_s.at[k, i], wp_r.at[k, i], col=partner)
+                copy.start()
+                waits.append(copy)
+
+    def weigh(source, held, tiles_high):
+        first_tile, stop = tiles_high
+        span = pl.ds(first_tile * TILE, (stop - first_tile) * TILE)
+        for i in range(own_blocks):
+            b = source * own_blocks + i
+            name = b.astype(jnp.float32)
+            side = i % 2
+            for t in range(first_tile, stop):
+                at = pl.ds(t * TILE, TILE)
+                if t < full:
+                    coef = Rows(lambda k, lanes: own_ref[k, at, lanes], slots)
+                else:
+                    coef = Rows(lambda k, lanes: lead_sc[k, :, lanes], slots)
+                top, low = split(select_block(coef, lambda k: label_own[k, at, :], name))
+                d_top[side, at, :] = top
+                d_low[side, at, :] = low
+            w_top, w_low = split(w_out[b] if held is None else held[i])
+            top, low = split(three(d_top[side, span, :], d_low[side, span, :], w_top, w_low, ((1,), (0,))))
+            g_top[b, span, :] = top
+            g_low[b, span, :] = low
+
+    weigh(c, w_ref, tiles_high=(0, full))
 
     relay_right = send(leads_out.at[c], leads_out.at[c], lead_s.at[0], lead_r.at[0], row=right)
     relay_left = send(leads_out.at[c], leads_out.at[c], lead_s.at[1], lead_r.at[0], row=left)
@@ -178,6 +222,9 @@
         if s < last or h == 1:
             send(tiles_out.at[behind, part[h]], tiles_out.at[behind, part[h]], bwd_s.at[s, h], bwd_r.at[s, h], row=left).start()
 
+    for i in range(own_blocks):
+        arrived(0, i)
+    weigh(partner, None, tiles_high=(0, full))
     pending = [(s, h) for s in range(1, half) for h in range(2)]
 
     def serve(count):
@@ -186,13 +233,7 @@
                 ring(*pending.pop(0))
 
     serve(2)
-    for k in range(1, cols // 2):
-        send(w_ref, w_out.at[pl.ds(c * own_blocks, own_blocks)], wx_s.at[k], wx_r.at[k], col=(c + 2 * k) % cols).wait_recv()
-        source = (c + cols - 2 * k) % cols
-        span = pl.ds(source * own_blocks, own_blocks)
-        copy = send(w_out.at[span], w_out.at[span], wp_s.at[k], wp_r.at[k], col=partner)
-        copy.start()
-        waits.append(copy)
+    forward(0)
     for d in range(1, cols):
         send(leads_out.at[c], leads_out.at[c], share_s.at[d], share_r.at[d], col=(c + d) % cols).wait_recv()
 
@@ -204,58 +245,69 @@
         send(names_ref, names_out.at[r], name_s.at[d], name_r.at[d], row=(r + d) % rows).wait_recv()
     for copy in own:
         copy.wait()
-    chunk = TILE // cols
     for q in range(cols):
         lead_sc[:, q * chunk:(q + 1) * chunk, :] = leads_out[q]
     put_labels(label_own, height, small_out[0:8, :])
-    for k in range(cols // 2):
-        send(w_ref, w_out.at[pl.ds(c * own_blocks, own_blocks)], wp_s.at[k], wp_r.at[k], col=partner).wait_recv()
+    forward(1)
+    weigh(c, w_ref, tiles_high=(full, full + 1))
+    weigh(partner, None, tiles_high=(full, full + 1))
     serve(1)
-
-    def weigh(b, carry):
-        name = b.astype(jnp.float32)
-        for t in range(height // TILE + 1):
-            at = pl.ds(t * TILE, TILE)
-            if t < height // TILE:
-                coef = Rows(lambda k, lanes: own_ref[k, at, lanes], slots)
-            else:
-                coef = Rows(lambda k, lanes: lead_sc[k, :, lanes], slots)
-            top, low = split(select_block(coef, lambda k: label_own[k, at, :], name))
-            d_top[at, :] = top
-            d_low[at, :] = low
-        w_top, w_low = split(w_out[b])
-        top, low = split(three(d_top[...], d_low[...], w_top, w_low, ((1,), (0,))))
-        g_top[b] = top
-        g_low[b] = low
-        return carry
-
-    middle = blocks // 2
-    lax.fori_loop(0, middle, weigh, 0)
+    for i in range(2, own_blocks):
+        forward(i)
+    for k in range(1, cols // 2):
+        weigh((c + cols - 2 * k) % cols, None, tiles_high=(0, full + 1))
+        serve(1)
+    for k in range(1, cols // 2):
+        for i in range(own_blocks):
+            arrived(k, i)
+        weigh((partner + cols - 2 * k) % cols, None, tiles_high=(0, full + 1))
     serve(1)
-    lax.fori_loop(middle, blocks, weigh, 0)
-    serve(1)
-
-    def group(tiles):
+
+    lane = lax.broadcasted_iota(jnp.int32, (TILE, TILE), 1)
+    line = lax.broadcasted_iota(jnp.int32, (TILE, TILE), 0)
+
+    def eliminate(j):
+        at = jnp.minimum(j, TILE - 1)
+        pivot = work[pl.ds(at, 1), :]
+        column = jnp.sum(jnp.where(lane == at, work[:, :TILE], 0.0), axis=1, keepdims=True)
+        scale = jnp.sum(jnp.where(lane[0:1] == at, pivot[:, :TILE], 0.0), axis=1, keepdims=True)
+        factor = jnp.where(line[:, 0:1] > j, column, 0.0) / scale
+        work[...] = work[...] - factor * pivot
+
+    fold = max(u for u in range(1, 5) if blocks % u == 0)
+    rounds = blocks // fold
+    steps = -(-TILE // ((half - 1) * rounds))
+
+    def group(tiles, step=None):
         width = len(tiles) * TILE
         for i, row in enumerate(tiles):
             put_labels(label_col, i * TILE, small_out[0:8, :] if row is None else names_out[row])
         acc[:, :width] = jnp.zeros((acc.shape[0], width), jnp.float32)
 
-        def body(b, carry):
-            name = b.astype(jnp.float32)
-            for i, row in enumerate(tiles):
-                at = pl.ds(i * TILE, TILE)
-                if row is None:
-                    coef = Rows(lambda k, lanes: lead_sc[k, :, lanes], slots)
-                else:
-                    coef = Rows(lambda k, lanes: tiles_out[row, k, :, lanes], slots)
-                top, low = split(select_block(coef, lambda k: label_col[k, at, :], name))
-                c_top[at, :] = top
-                c_low[at, :] = low
-            acc[:, :width] += three(g_top[b], g_low[b], c_top[:width, :], c_low[:width, :], ((1,), (1,)))
+        def body(n, carry):
+            for u in range(fold):
+                name = (n * fold + u).astype(jnp.float32)
+                for i, row in enumerate(tiles):
+                    at = pl.ds(i * TILE, TILE)
+                    if row is None:
+                        coef = Rows(lambda k, lanes: lead_sc[k, :, lanes], slots)
+                    else:
+                        coef = Rows(lambda k, lanes: tiles_out[row, k, :, lanes], slots)
+                    top, low = split(select_block(coef, lambda k: label_col[k, at, :], name))
+                    c_top[u, at, :] = top
+                    c_low[u, at, :] = low
+            a_top = [g_top[n * fold + u] for u in range(fold)]
+            a_low = [g_low[n * fold + u] for u in range(fold)]
+            b_top = [c_top[u, :width, :] for u in range(fold)]
+            b_low = [c_low[u, :width, :] for u in range(fold)]
+            acc[:, :width] += product(
+                jnp.concatenate(a_top + a_top + a_low, axis=1), jnp.concatenate(b_top + b_low + b_top, axis=1), ((1,), (1,)))
+            if step is not None:
+                for e in range(steps):
+                    eliminate(step + n * steps + e)
             return carry
 
-        lax.fori_loop(0, blocks, body, 0)
+        lax.fori_loop(0, rounds, body, 0)
         for i, row in enumerate(tiles):
             value = acc[:, i * TILE:(i + 1) * TILE]
             if row is None:
@@ -266,32 +318,18 @@
     group([None, r])
     serve(1)
 
-    lane = lax.broadcasted_iota(jnp.int32, (TILE, TILE), 1)
-    line = lax.broadcasted_iota(jnp.int32, (TILE, TILE), 0)
     work[:, :TILE] = lead_schur_out[height:, :] + jnp.where(lane == line, jnp.broadcast_to(small_out[7:8, :], (TILE, TILE)), 0.0)
     work[:, TILE:] = jnp.where(lane == line, 1.0, 0.0)
-
-    def eliminate(j, carry):
-        pivot = work[pl.ds(j, 1), :]
-        column = jnp.sum(jnp.where(lane == j, work[:, :TILE], 0.0), axis=1, keepdims=True)
-        scale = jnp.sum(jnp.where(lane[0:1] == j, pivot[:, :TILE], 0.0), axis=1, keepdims=True)
-        factor = jnp.where(line[:, 0:1] > j, column, 0.0) / scale
-        work[...] = work[...] - factor * pivot
-        return carry
-
-    lax.fori_loop(0, TILE // 2, eliminate, 0)
-    serve(1)
-    lax.fori_loop(TILE // 2, TILE, eliminate, 0)
-    diagonal = jnp.sum(jnp.where(lane == line, work[:, :TILE], 0.0), axis=1, keepdims=True)
-    inverse_out[...] = work[:, TILE:] / jnp.sqrt(diagonal)
 
     for g in range(1, half):
         while pending and pending[0][0] <= g:
             serve(1)
-        group([row_at(pos - g), row_at(pos + g)])
+        group([row_at(pos - g), row_at(pos + g)], (g - 1) * rounds * steps)
         serve(2)
     send(tile_ref.at[part[0]], tiles_out.at[r, part[0]], fwd_s.at[last, 0], fwd_r.at[last, 0], row=right).wait_recv()
     send(tile_ref.at[part[1]], tiles_out.at[r, part[1]], bwd_s.at[last, 1], bwd_r.at[last, 1], row=left).wait_recv()
+    diagonal = jnp.sum(jnp.where(lane == line, work[:, :TILE], 0.0), axis=1, keepdims=True)
+    inverse_out[...] = work[:, TILE:] / jnp.sqrt(diagonal)
     group([row_at(pos + half)])
 
     for s in range(half):
@@ -319,7 +357,7 @@
         relay_left.wait_send()
 
 
-def assemble(rows, cols, tile, names, lead, small, weights, own, own_names):
+def assemble(rows, cols, small, weights, own, own_names):
     half = rows // 2
     dma = pltpu.SemaphoreType.DMA
     vmem = pl.BlockSpec(memory_space=pltpu.VMEM)
@@ -335,29 +373,29 @@
             jax.ShapeDtypeStruct((TILE, TILE), f32),
             jax.ShapeDtypeStruct(small.shape, f32),
         ],
-        in_specs=[vmem] * 7,
+        in_specs=[vmem] * 4,
         out_specs=[vmem] * 4,
         scratch_shapes=[
-            pltpu.VMEM((rows,) + tile.shape, f32),
-            pltpu.VMEM((rows,) + names.shape, f32),
-            pltpu.VMEM((cols,) + lead.shape, f32),
+            pltpu.VMEM((rows, slots, TILE, order), f32),
+            pltpu.VMEM((rows,) + own_names.shape[1:], f32),
+            pltpu.VMEM((cols, slots, TILE // cols, order), f32),
             pltpu.VMEM((blocks, order, order), f32),
             pltpu.VMEM((slots, tall, TILE), f32),
             pltpu.VMEM((slots, 2 * TILE, TILE), f32),
             pltpu.VMEM((slots, TILE, order), f32),
-            pltpu.VMEM((tall, order), bf16),
-            pltpu.VMEM((tall, order), bf16),
-            pltpu.VMEM((2 * TILE, order), bf16),
-            pltpu.VMEM((2 * TILE, order), bf16),
+            pltpu.VMEM((2, tall, order), bf16),
+            pltpu.VMEM((2, tall, order), bf16),
+            pltpu.VMEM((4, 2 * TILE, order), bf16),
+            pltpu.VMEM((4, 2 * TILE, order), bf16),
             pltpu.VMEM((blocks, tall, order), bf16),
             pltpu.VMEM((blocks, tall, order), bf16),
             pltpu.VMEM((tall, 2 * TILE), f32),
             pltpu.VMEM((TILE, 2 * TILE), f32),
         ]
         + [dma((5,))] + [dma((half, 2))] * 4 + [dma((rows,))] * 2 + [dma((2,)), dma((1,))]
-        + [dma((cols,))] * 2 + [dma((rows,)), dma((1,))] + [dma((cols,))] * 4,
+        + [dma((cols,))] * 2 + [dma((rows,)), dma((1,))] + [dma((cols, weights.shape[0]))] * 4,
         compiler_params=pltpu.CompilerParams(collective_id=0, has_side_effects=True),
-    )(tile, names, lead, small, weights, own, own_names)
+    )(small, weights, own, own_names)
 
 
 def local(coefficients, support, primal, dual_inverse, block_sizes, damping, right_sides):
@@ -374,18 +412,13 @@
     active = (positions[None, :] < block_sizes[:, None]).astype(jnp.float32)
     weights = primal * dual_inverse * active[:, :, None] * active[:, None, :]
 
-    layer = (col_index * col_width) // span
-    tile = jnp.transpose(lax.dynamic_index_in_dim(coefficients, layer, 0, keepdims=False), (1, 0, 2))
     own_names = jnp.pad(jnp.transpose(support, (0, 2, 1)).astype(jnp.float32), ((0, 0), (0, 8 - slots), (0, 0)))
-    names = lax.dynamic_index_in_dim(own_names, layer, 0, keepdims=False)
-    chunk = TILE // cols
-    lead = jnp.transpose(lax.dynamic_slice_in_dim(coefficients[0], col_index * chunk, chunk, 0), (1, 0, 2))
     small = jnp.concatenate([
         own_names[0][:7],
         damping[0][None, :],
         jnp.pad(right_sides[0], ((0, -sides % 8), (0, 0)))], axis=0)
     own = jnp.transpose(coefficients, (2, 0, 1, 3)).reshape(slots, layers * TILE, order)
-    schur_rows, own_lead, inverse, small = assemble(rows, cols, tile, names, lead, small, weights, own, own_names)
+    schur_rows, own_lead, inverse, small = assemble(rows, cols, small, weights, own, own_names)
     if span != col_width:
         schur_rows = lax.dynamic_slice_in_dim(schur_rows, (col_index * col_width) % span, col_width, 1)
     lead_damping = small[7]

time: 109 us -> 91.8 us (0.84); the launches traced: 107 us -> 91.4 us
  Pallas kernels: 87.4 us -> 72.4 us
    pallas_call x1, Pallas kernels: 87.4 us -> 72.4 us  [assemble(): pl.pallas_call(functools.partial(exchange, rows, cols), out_shape=[jax.Sh...]
    transpose x1, local copies, waits for them, and re-layouts: 1.7 us -> 3.43 us  [local(): jnp.transpose(coefficients, (2, 0, 1, 3))]
    dynamic_slice x3 -> x0, local copies, waits for them, and re-layouts: 1.58 us -> none  [the longest x1 0.89 us: local(): lax.dynamic_index_in_dim(coefficients, layer, 0, keepdims=False)]
    slice x1 -> x0, local copies, waits for them, and re-layouts: 1.52 us -> none  [local(): coefficients[0]]
where the time goes in v1:
time: 91.8 us; the launch traced here: 91.4 us
  Pallas kernels  72.4 us (79%)
  matrix products  9.49 us (10%)
  local copies, waits for them, and re-layouts  6.13 us (7%)
  other arithmetic  2.69 us (3%)
    pallas_call x1, Pallas kernels, assemble(): pl.pallas_call(functools.partial(exchange, rows, cols), out_shape=[jax.Sh...  72.4 us
    dot_general x1, matrix products, local(): outer_term = jnp.dot(panel_factor, column_panel, precision=highest)  5.13 us
    transpose x1, local copies, waits for them, and re-layouts, local(): jnp.transpose(coefficients, (2, 0, 1, 3))  3.43 us

profile of v1, /device:TPU:22, one launch (start us, length us, event | category | flops | bytes accessed | tf_op | source)
XLA Modules:
  0.0 91.4 jit_solution(263258066450005875)
XLA Ops:
  0.6 0.7 convert_bitcast_fusion
  1.3 0.7 slice_bitcast_fusion
  2.0 0.7 slice.31
  2.7 0.6 pad_maximum_fusion.small_ref
  3.3 0.6 pad.4.own_names_ref
  3.9 0.0 copy-start.7
  3.9 0.0 copy-start.1
  3.9 0.0 copy-start.2
  3.9 3.4 %copy.10 = f32[4,4,128,256]{3,2,1,0:T(8,128)} copy(f32[4,4,128,256]{3,0,2,1:T(4,128)} %bitcast.35) | data formatting | bytes 4194304 | tf_op jit(solution)/shard_map/transpose | solution.py:420
  7.4 0.0 copy-done.7
  7.4 0.1 fusion.19
  7.4 0.0 copy-done.1
  7.4 0.0 copy-done.2
  7.4 1.1 %multiply_multiply_fusion.w_ref = f32[3,256,256]{2,1,0:T(8,128)} fusion(f32[3,256,256]{2,1,0:T(8,128)S(1)} %copy-done.1, f32[3,256,256]{2,1,0:T(8,128)S(1)} %copy-done.2, f32[3,256]{1,0:T(4,128)S(1)} %fusion.19), kind=kLoop, calls=%fused_computation.4 | loop fusion | flops 589824 | bytes 2362368 | tf_op jit(solution)/shard_map/mul | solution.py:413
  8.5 0.0 copy-start.5
  8.5 72.4 %shard_map.94 = (f32[640,1024]{1,0:T(8,128)}, f32[640,128]{1,0:T(8,128)}, f32[128,128]{1,0:T(8,128)}, f32[16,128]{1,0:T(8,128)}) custom-call(f32[16,128]{1,0:T(8,128)} %pad_maximum_fusion.small_ref, f32[3,256,256]{2,1,0:T(8,128)} %multiply_multiply_fusion.w_ref, f32[4,512,256]{2,1,0:T(8,128)} %bitcast.32, f32[4,8,128]{2,1,0:T(8,128)} %pad.4.own_names_ref), custom_call_target="tpu_custom_call" | custom-call | tf_op jit(solution)/shard_map/pallas_call | solution.py:368
  80.9 0.7 slice_bitcast_fusion.2
  81.6 1.8 %fusion.2 = f32[128,1024]{1,0:T(8,128)S(1)} fusion(f32[128,128]{1,0:T(8,128)} %get-tuple-element.9, f32[640,1024]{1,0:T(8,128)} %get-tuple-element.7, f32[128]{0:T(128)S(1)} %slice_bitcast_fusion.2, s32[1024]{0:T(1024)S(1)} %iota_add_fusion), kind=kOutput, calls=%fused_computation.5 | convolution fusion | flops 201719808 | bytes 1118720 | tf_op jit(solution)/shard_map/jk,kn->jn/dot_general | solution.py:435
  83.4 0.1 fusion.21
  83.5 0.0 copy-done.5
  83.5 1.4 %fusion.9 = f32[512,128]{1,0:T(8,128)S(1)} fusion(f32[128,128]{1,0:T(8,128)} %get-tuple-element.9, f32[640,128]{1,0:T(8,128)} %get-tuple-element.8, f32[512]{0:T(512)S(1)} %bitcast.37, s32[512]{0:T(512)S(1)} %fusion.21), kind=kOutput, calls=%fused_computation.13 | convolution fusion | flops 100859904 | bytes 593920 | tf_op jit(solution)/shard_map/ak,jk->aj/dot_general | solution.py:434
  84.9 0.0 copy-start
  84.9 0.1 broadcast_compare_fusion.1
  85.0 0.0 copy-start.3
  85.0 0.0 copy-start.6
  85.0 0.0 copy-start.4
  85.0 5.1 %select_subtract_fusion = f32[512,1024]{1,0:T(8,128)} fusion(f32[640,1024]{1,0:T(8,128)} %get-tuple-element.7, f32[512,128]{1,0:T(8,128)S(1)} %fusion.9, f32[128,1024]{1,0:T(8,128)S(1)} %fusion.2, f32[512]{0:T(512)S(1)} %bitcast.38, s32[1024]{0:T(1024)S(1)} %iota_add_fusion, s32[512]{0:T(512)S(1)} %fusion.21, pred[1024]{0:T(1024)(128)(4,1)S(1)} %broadcast_compare_fusion, ...), kind=kOutput, calls=%fused_computation | convolution fusion | flops 808452096 | bytes 4990464 | tf_op jit(solution)/shard_map/dot_general | solution.py:436
  90.2 0.0 copy-done.3
  90.2 0.0 copy-done.6
  90.2 0.2 fusion.17
  90.3 0.1 fusion.20
  90.4 0.0 copy-done
  90.4 0.0 copy-done.4
  90.4 1.0 %fusion.1 = f32[4,8,128]{2,1,0:T(8,128)} fusion(f32[4,8,128]{2,1,0:T(8,128)S(1)} %copy-done.4, f32[4,128,128]{2,1,0:T(8,128)S(1)} %bitcast.33, f32[8,128]{1,0:T(8,128)S(1)} %fusion.17, pred[4,128]{1,0:T(4,128)(4,1)S(1)} %fusion.20), kind=kOutput, calls=%fused_computation.3 | convolution fusion | flops 6299648 | bytes 299520 | tf_op jit(solution)/shard_map/sk,tak->tsa/dot_general | solution.py:442
  (4 shorter events, 0.0 us)
Async XLA Ops:
  3.9 3.4 %copy-start.7 = (s32[3]{0:T(128)S(1)}, s32[3]{0:T(128)}, u32[]{:S(2)}) copy-start(s32[3]{0:T(128)} %param.11) | copy-start | bytes 40
  3.9 3.5 %copy-start.1 = (f32[3,256,256]{2,1,0:T(8,128)S(1)}, f32[3,256,256]{2,1,0:T(8,128)}, u32[]{:S(2)}) copy-start(f32[3,256,256]{2,1,0:T(8,128)} %param.9) | copy-start | bytes 2359300
  3.9 3.5 %copy-start.2 = (f32[3,256,256]{2,1,0:T(8,128)S(1)}, f32[3,256,256]{2,1,0:T(8,128)}, u32[]{:S(2)}) copy-start(f32[3,256,256]{2,1,0:T(8,128)} %param.10) | copy-start | bytes 2359300
  8.5 75.0 %copy-start.5 = (f32[4,128]{1,0:T(4,128)S(1)}, f32[4,128]{1,0:T(4,128)}, u32[]{:S(2)}) copy-start(f32[4,128]{1,0:T(4,128)} %param.12) | copy-start | bytes 6148
  84.9 5.5 %copy-start = (f32[512,128]{1,0:T(8,128)}, f32[512,128]{1,0:T(8,128)S(1)}, u32[]{:S(2)}) copy-start(f32[512,128]{1,0:T(8,128)S(1)} %fusion.9) | copy-start | bytes 786436
  85.0 5.2 %copy-start.3 = (f32[128,128]{1,0:T(8,128)S(1)}, f32[128,128]{1,0:T(8,128)}, u32[]{:S(2)}) copy-start(f32[128,128]{1,0:T(8,128)} %get-tuple-element.9) | copy-start | bytes 196612
  85.0 5.2 %copy-start.6 = (f32[16,128]{1,0:T(8,128)S(1)}, f32[16,128]{1,0:T(8,128)}, u32[]{:S(2)}) copy-start(f32[16,128]{1,0:T(8,128)} %get-tuple-element.10) | copy-start | bytes 24580
  85.0 5.4 %copy-start.4 = (f32[4,8,128]{2,1,0:T(8,128)S(1)}, f32[4,8,128]{2,1,0:T(8,128)}, u32[]{:S(2)}) copy-start(f32[4,8,128]{2,1,0:T(8,128)} %param.13) | copy-start | bytes 49156

commit v2 on v1

--- a/solution.py
+++ b/solution.py
@@ -261,7 +261,6 @@
         for i in range(own_blocks):
             arrived(k, i)
         weigh((partner + cols - 2 * k) % cols, None, tiles_high=(0, full + 1))
-    serve(1)
 
     lane = lax.broadcasted_iota(jnp.int32, (TILE, TILE), 1)
     line = lax.broadcasted_iota(jnp.int32, (TILE, TILE), 0)
@@ -325,7 +324,7 @@
         while pending and pending[0][0] <= g:
             serve(1)
         group([row_at(pos - g), row_at(pos + g)], (g - 1) * rounds * steps)
-        serve(2)
+        serve(1)
     send(tile_ref.at[part[0]], tiles_out.at[r, part[0]], fwd_s.at[last, 0], fwd_r.at[last, 0], row=right).wait_recv()
     send(tile_ref.at[part[1]], tiles_out.at[r, part[1]], bwd_s.at[last, 1], bwd_r.at[last, 1], row=left).wait_recv()
     diagonal = jnp.sum(jnp.where(lane == line, work[:, :TILE], 0.0), axis=1, keepdims=True)

time: 91.8 us -> 86.5 us (0.942)
  Pallas kernels: 72.4 us -> 67.1 us
    pallas_call x1, Pallas kernels: 72.4 us -> 67.1 us  [assemble(): pl.pallas_call(functools.partial(exchange, rows, cols), out_shape=[jax.Sh...]
where the time goes in v2:
time: 86.5 us; the launch traced here: 86.1 us
  Pallas kernels  67.1 us (78%)
  matrix products  9.49 us (11%)
  local copies, waits for them, and re-layouts  6.13 us (7%)
  other arithmetic  2.69 us (3%)
    pallas_call x1, Pallas kernels, assemble(): pl.pallas_call(functools.partial(exchange, rows, cols), out_shape=[jax.Sh...  67.1 us
    dot_general x1, matrix products, local(): outer_term = jnp.dot(panel_factor, column_panel, precision=highest)  5.13 us
    transpose x1, local copies, waits for them, and re-layouts, local(): jnp.transpose(coefficients, (2, 0, 1, 3))  3.43 us
    dot_general x1, matrix products, local(): jnp.einsum('jk,kn->jn', inverse, column_raw, precision=highest)  1.78 us

profile of v2, /device:TPU:22, one launch (start us, length us, event | category | flops | bytes accessed | tf_op | source)
XLA Modules:
  0.0 86.1 jit_solution(1125252558017889981)
XLA Ops:
  0.6 0.7 convert_bitcast_fusion
  1.3 0.7 slice_bitcast_fusion
  2.0 0.7 slice.31
  2.7 0.6 pad_maximum_fusion.small_ref
  3.3 0.6 pad.4.own_names_ref
  3.9 0.0 copy-start.7
  3.9 0.0 copy-start.1
  3.9 0.0 copy-start.2
  3.9 3.4 %copy.10 = f32[4,4,128,256]{3,2,1,0:T(8,128)} copy(f32[4,4,128,256]{3,0,2,1:T(4,128)} %bitcast.35) | data formatting | bytes 4194304 | tf_op jit(solution)/shard_map/transpose | solution.py:419
  7.4 0.0 copy-done.7
  7.4 0.1 fusion.19
  7.4 0.0 copy-done.1
  7.4 0.0 copy-done.2
  7.4 1.1 %multiply_multiply_fusion.w_ref = f32[3,256,256]{2,1,0:T(8,128)} fusion(f32[3,256,256]{2,1,0:T(8,128)S(1)} %copy-done.1, f32[3,256,256]{2,1,0:T(8,128)S(1)} %copy-done.2, f32[3,256]{1,0:T(4,128)S(1)} %fusion.19), kind=kLoop, calls=%fused_computation.4 | loop fusion | flops 589824 | bytes 2362368 | tf_op jit(solution)/shard_map/mul | solution.py:412
  8.5 0.0 copy-start.5
  8.5 67.1 %shard_map.94 = (f32[640,1024]{1,0:T(8,128)}, f32[640,128]{1,0:T(8,128)}, f32[128,128]{1,0:T(8,128)}, f32[16,128]{1,0:T(8,128)}) custom-call(f32[16,128]{1,0:T(8,128)} %pad_maximum_fusion.small_ref, f32[3,256,256]{2,1,0:T(8,128)} %multiply_multiply_fusion.w_ref, f32[4,512,256]{2,1,0:T(8,128)} %bitcast.32, f32[4,8,128]{2,1,0:T(8,128)} %pad.4.own_names_ref), custom_call_target="tpu_custom_call" | custom-call | tf_op jit(solution)/shard_map/pallas_call | solution.py:367
  75.6 0.7 slice_bitcast_fusion.2
  76.3 1.8 %fusion.2 = f32[128,1024]{1,0:T(8,128)S(1)} fusion(f32[128,128]{1,0:T(8,128)} %get-tuple-element.9, f32[640,1024]{1,0:T(8,128)} %get-tuple-element.7, f32[128]{0:T(128)S(1)} %slice_bitcast_fusion.2, s32[1024]{0:T(1024)S(1)} %iota_add_fusion), kind=kOutput, calls=%fused_computation.5 | convolution fusion | flops 201719808 | bytes 1118720 | tf_op jit(solution)/shard_map/jk,kn->jn/dot_general | solution.py:434
  78.1 0.1 fusion.21
  78.2 0.0 copy-done.5
  78.2 1.4 %fusion.9 = f32[512,128]{1,0:T(8,128)S(1)} fusion(f32[128,128]{1,0:T(8,128)} %get-tuple-element.9, f32[640,128]{1,0:T(8,128)} %get-tuple-element.8, f32[512]{0:T(512)S(1)} %bitcast.37, s32[512]{0:T(512)S(1)} %fusion.21), kind=kOutput, calls=%fused_computation.13 | convolution fusion | flops 100859904 | bytes 593920 | tf_op jit(solution)/shard_map/ak,jk->aj/dot_general | solution.py:433
  79.6 0.0 copy-start
  79.6 0.1 broadcast_compare_fusion.1
  79.7 0.0 copy-start.3
  79.7 0.0 copy-start.6
  79.7 0.0 copy-start.4
  79.7 5.1 %select_subtract_fusion = f32[512,1024]{1,0:T(8,128)} fusion(f32[640,1024]{1,0:T(8,128)} %get-tuple-element.7, f32[512,128]{1,0:T(8,128)S(1)} %fusion.9, f32[128,1024]{1,0:T(8,128)S(1)} %fusion.2, f32[512]{0:T(512)S(1)} %bitcast.38, s32[1024]{0:T(1024)S(1)} %iota_add_fusion, s32[512]{0:T(512)S(1)} %fusion.21, pred[1024]{0:T(1024)(128)(4,1)S(1)} %broadcast_compare_fusion, ...), kind=kOutput, calls=%fused_computation | convolution fusion | flops 808452096 | bytes 4990464 | tf_op jit(solution)/shard_map/dot_general | solution.py:435
  84.8 0.0 copy-done.3
  84.8 0.0 copy-done.6
  84.8 0.2 fusion.17
  85.0 0.1 fusion.20
  85.1 0.0 copy-done
  85.1 0.0 copy-done.4
  85.1 1.0 %fusion.1 = f32[4,8,128]{2,1,0:T(8,128)} fusion(f32[4,8,128]{2,1,0:T(8,128)S(1)} %copy-done.4, f32[4,128,128]{2,1,0:T(8,128)S(1)} %bitcast.33, f32[8,128]{1,0:T(8,128)S(1)} %fusion.17, pred[4,128]{1,0:T(4,128)(4,1)S(1)} %fusion.20), kind=kOutput, calls=%fused_computation.3 | convolution fusion | flops 6299648 | bytes 299520 | tf_op jit(solution)/shard_map/sk,tak->tsa/dot_general | solution.py:441
  (4 shorter events, 0.0 us)
Async XLA Ops:
  3.9 3.4 %copy-start.7 = (s32[3]{0:T(128)S(1)}, s32[3]{0:T(128)}, u32[]{:S(2)}) copy-start(s32[3]{0:T(128)} %param.11) | copy-start | bytes 40
  3.9 3.5 %copy-start.1 = (f32[3,256,256]{2,1,0:T(8,128)S(1)}, f32[3,256,256]{2,1,0:T(8,128)}, u32[]{:S(2)}) copy-start(f32[3,256,256]{2,1,0:T(8,128)} %param.9) | copy-start | bytes 2359300
  3.9 3.5 %copy-start.2 = (f32[3,256,256]{2,1,0:T(8,128)S(1)}, f32[3,256,256]{2,1,0:T(8,128)}, u32[]{:S(2)}) copy-start(f32[3,256,256]{2,1,0:T(8,128)} %param.10) | copy-start | bytes 2359300
  8.5 69.6 %copy-start.5 = (f32[4,128]{1,0:T(4,128)S(1)}, f32[4,128]{1,0:T(4,128)}, u32[]{:S(2)}) copy-start(f32[4,128]{1,0:T(4,128)} %param.12) | copy-start | bytes 6148
  79.6 5.5 %copy-start = (f32[512,128]{1,0:T(8,128)}, f32[512,128]{1,0:T(8,128)S(1)}, u32[]{:S(2)}) copy-start(f32[512,128]{1,0:T(8,128)S(1)} %fusion.9) | copy-start | bytes 786436
  79.7 5.2 %copy-start.3 = (f32[128,128]{1,0:T(8,128)S(1)}, f32[128,128]{1,0:T(8,128)}, u32[]{:S(2)}) copy-start(f32[128,128]{1,0:T(8,128)} %get-tuple-element.9) | copy-start | bytes 196612
  79.7 5.2 %copy-start.6 = (f32[16,128]{1,0:T(8,128)S(1)}, f32[16,128]{1,0:T(8,128)}, u32[]{:S(2)}) copy-start(f32[16,128]{1,0:T(8,128)} %get-tuple-element.10) | copy-start | bytes 24580
  79.7 5.4 %copy-start.4 = (f32[4,8,128]{2,1,0:T(8,128)S(1)}, f32[4,8,128]{2,1,0:T(8,128)}, u32[]{:S(2)}) copy-start(f32[4,8,128]{2,1,0:T(8,128)} %param.13) | copy-start | bytes 49156
